TPU v7x, 512 devices: a whole 4x4x16 slice. The times are simulated.
512 devices in a mesh: fsdp: 32 (over y, z_lo, core), head: 4 (over z_hi), seq: 4 (over x).
Axes of the slice: x: 4, y: 4, z: 16 (z_hi: 4, z_lo: 4; z = z_hi * 4 + z_lo), core: 2. Of those that a mesh axis runs over, the one named last changes fastest.
Arguments:
- latents: bfloat16 [6144, 6144], P('fsdp', ('head', 'seq')), may hold values from -100 to 100
- train_qkv: bfloat16 [3, 6144, 4096], P(None, 'fsdp', ('head', 'seq')), may hold values from -0.078125 to 0.078125
- ema_qkv: bfloat16 [3, 6144, 4096], P(None, 'fsdp', ('head', 'seq')), may hold values from -0.078125 to 0.078125
- q_gain: float32 [128], replicated, may hold values from 0.8 to 2.5
- k_gain: float32 [128], replicated, may hold values from 0.8 to 2.5
- out_weight: bfloat16 [4096, 6144], P(('head', 'seq')), may hold values from -0.125 to 0.125
- modulation: float32 [8, 3, 6144], replicated, may hold values from -4 to 4
- timestep: int32 [1], replicated, may hold values from 0 to 7
- step: int32 [1], replicated, may hold values from 0 to 7
Outputs:
- block_output: bfloat16 [6144, 6144], P('fsdp', ('head', 'seq'))
All inputs are finite; a program needn't handle non-finite values.
Results may differ from a plain program's by a relative error of at most 0.025.
Values may be sent and summed in bfloat16 or wider, within the bound.
No kernel may reach another device: no remote copies, remote signals or barrier semaphores. Data moves between devices by JAX's collectives and lax.ppermute only.
A program may use at most 64 MiB of HBM per device.

v0:
```python
import math
import jax
import jax.numpy as jnp
from jax import lax
from jax.sharding import PartitionSpec as P

D = 6144
HD = 128


def head_norm(projected_part, gain, heads):
    shaped = projected_part.reshape(projected_part.shape[0], heads, HD)
    squares = jnp.mean(shaped * shaped, axis=2, keepdims=True)
    return (shaped * lax.rsqrt(squares + 1e-06) * gain).astype(jnp.bfloat16)


def per_device(latents, train_qkv, ema_qkv, q_gain, k_gain, out_weight, modulation, timestep, step):
    rows_here = latents.shape[0]
    local_width = latents.shape[1]
    channels = ema_qkv.shape[2]
    heads = channels // HD
    stepped = step[0].astype(jnp.float32)
    decay = (1.0 + stepped) / (10.0 + stepped)
    ema_weights = (
        decay * ema_qkv.astype(jnp.float32) + (1.0 - decay) * train_qkv.astype(jnp.float32)
    ).astype(jnp.bfloat16)
    chosen = (jnp.arange(modulation.shape[0], dtype=jnp.int32) == timestep[0]).astype(jnp.float32)
    mod_row = jnp.einsum("n,ncd->cd", chosen, modulation, precision=lax.Precision.HIGHEST)
    position = lax.axis_index(("head", "seq")) * local_width
    own_mod = lax.dynamic_slice_in_dim(mod_row, position, local_width, 1)
    widened = latents.astype(jnp.float32)
    average = lax.psum(jnp.sum(widened, axis=1), ("head", "seq")) / D
    centred = widened - average[:, None]
    variance = lax.psum(jnp.sum(centred * centred, axis=1), ("head", "seq")) / D
    shares = (
        centred * lax.rsqrt(variance + 1e-06)[:, None] * (1.0 + own_mod[1]) + own_mod[0]
    ).astype(jnp.bfloat16)
    hidden = lax.all_gather(shares, ("head", "seq"), axis=1, tiled=True)
    full_weights = lax.all_gather(ema_weights, "fsdp", axis=1, tiled=True)
    projected = jnp.einsum("td,jdh->jth", hidden, full_weights, preferred_element_type=jnp.float32)
    queries = head_norm(projected[0], q_gain, heads)
    keys = head_norm(projected[1], k_gain, heads).reshape(rows_here, channels)
    values = projected[2].astype(jnp.bfloat16)
    scaling = 1.0 / math.sqrt(HD)

    def one_block(carry, operands):
        numer, totals = carry
        key_block, value_block = operands
        scores = (
            jnp.einsum("qhd,khd->hqk", queries, key_block, preferred_element_type=jnp.float32)
            * scaling
        )
        expo = jnp.exp(scores)
        weights = expo.astype(jnp.bfloat16)
        numer = numer + jnp.einsum(
            "hqk,khd->qhd", weights, value_block, preferred_element_type=jnp.float32
        )
        totals = totals + jnp.transpose(jnp.sum(expo, axis=2))
        return ((numer, totals), None)

    starting_numer = jnp.zeros((rows_here, heads, HD), jnp.float32)
    starting_totals = jnp.zeros((rows_here, heads), jnp.float32)
    carry = (starting_numer, starting_totals)
    pieces = (
        lax.all_gather(keys, "fsdp", axis=0, tiled=True),
        lax.all_gather(values, "fsdp", axis=0, tiled=True),
    )
    piece_rows = pieces[0].shape[0]
    block_rows = math.gcd(piece_rows, 512)
    count = piece_rows // block_rows
    key_blocks = pieces[0].reshape(count, block_rows, heads, HD)
    value_blocks = pieces[1].reshape(count, block_rows, heads, HD)
    carry, _ = lax.scan(one_block, carry, (key_blocks, value_blocks))
    numer, totals = carry
    attended = (numer / totals[:, :, None]).astype(jnp.bfloat16).reshape(rows_here, channels)
    partial_terms = jnp.dot(attended, out_weight, preferred_element_type=jnp.float32).astype(
        jnp.bfloat16
    )
    summed = lax.psum(partial_terms, ("head", "seq")).astype(jnp.float32)
    branch = lax.dynamic_slice_in_dim(summed, position, local_width, 1)
    return (widened + own_mod[2][None, :] * branch).astype(jnp.bfloat16)


def solution(mesh):
    in_specs = (
        P("fsdp", ("head", "seq")),
        P(None, "fsdp", ("head", "seq")),
        P(None, "fsdp", ("head", "seq")),
        P(),
        P(),
        P(("head", "seq"), None),
        P(),
        P(),
        P(),
    )
    out_specs = P("fsdp", ("head", "seq"))
    return jax.shard_map(
        per_device, mesh=mesh, in_specs=in_specs, out_specs=out_specs, check_vma=False
    )
```

profile of v0, /device:TPU:40, one launch (start us, length us, event | category | flops | bytes accessed | tf_op | source)
XLA Modules:
  0.0 781.6 jit_solution(2207394032525884099)
XLA Ops:
  10.0 58.4 %psum.21 = f32[192]{0:T(256)S(1)} all-reduce(f32[192]{0:T(256)S(1)} %convert_reduce_fusion), channel_id=1, replica_groups=mesh['fsdp'=32,'head'=4,'seq'=4] {'head','seq'}, use_global_device_ids=true, to_apply=%region_1.0 | all-reduce | flops 192 | bytes 1536 | tf_op jit(solution)/shard_map/psum | solution.py:32
  69.5 46.3 %psum.22 = f32[192]{0:T(256)S(1)} all-reduce(f32[192]{0:T(256)S(1)} %fusion.11), channel_id=1, replica_groups=mesh['fsdp'=32,'head'=4,'seq'=4] {'head','seq'}, use_global_device_ids=true, to_apply=%region_3.0 | all-reduce | flops 192 | bytes 1536 | tf_op jit(solution)/shard_map/psum | solution.py:34
  121.0 85.2 %all-gather.8.cloned.1.call-done = bf16[192,6144]{1,0:T(8,128)(2,1)} async-done(((bf16[192,384]{1,0:T(8,128)(2,1)}), bf16[192,6144]{1,0:T(8,128)(2,1)}) %all-gather.8.cloned.1.call-update) | async-done | bytes 2359312 | tf_op jit(solution)/shard_map/all_gather | solution.py:38
  206.2 81.8 %all-gather.6.cloned.1.call-done = bf16[3,6144,256]{2,1,0:T(8,128)(2,1)} async-done(((bf16[3,192,256]{2,1,0:T(8,128)(2,1)}), bf16[3,6144,256]{2,1,0:T(8,128)(2,1)}) %all-gather.6.cloned.1.call-update) | async-done | bytes 9437200 | tf_op jit(solution)/shard_map/all_gather | solution.py:39
  287.9 6.4 fusion.6
  302.9 63.6 %all-gather.10.cloned.1.call-done = bf16[6144,256]{1,0:T(8,128)(2,1)} async-done(((bf16[192,256]{1,0:T(8,128)(2,1)}), bf16[6144,256]{1,0:T(8,128)(2,1)}) %all-gather.10.cloned.1.call-update) | async-done | bytes 3145744 | tf_op jit(solution)/shard_map/all_gather | solution.py:65
  366.5 5.5 reshape.43
  372.0 62.2 %all-gather.12.cloned.1.call-done = bf16[1,6144,256]{2,1,0:T(8,128)(2,1)} async-done(((bf16[1,192,256]{2,1,0:T(8,128)(2,1)}), bf16[1,6144,256]{2,1,0:T(8,128)(2,1)}) %all-gather.12.cloned.1.call-update) | async-done | bytes 3145744 | tf_op jit(solution)/shard_map/all_gather | solution.py:66
  434.2 5.5 reshape.42
  439.7 53.4 %while.13 = (s32[]{:T(128)}, f32[192,2,128]{2,0,1:T(8,128)}, f32[192,2]{0,1:T(2,128)S(1)}, bf16[12,512,2,128]{3,2,1,0:T(2,128)(2,1)}, bf16[12,512,2,128]{3,2,1,0...) while((s32[]{:T(128)}, f32[192,2,128]{2,0,1:T(8,128)}, ...), condition=%wide.region_8.9_spmd.clone, body=%wide.region_6.8_spmd.clone.sunk | while | flops 101351808 | bytes 2857060 | solution.py:73
  442.2 1.9 fusion.45
  446.6 2.0 fusion.45
  451.0 2.0 fusion.45
  455.5 2.0 fusion.45
  459.9 2.0 fusion.45
  464.4 2.0 fusion.45
  468.9 2.0 fusion.45
  473.3 2.0 fusion.45
  477.8 2.0 fusion.45
  482.2 2.0 fusion.45
  486.7 2.0 fusion.45
  491.1 2.0 fusion.45
  493.1 3.2 convolution_convert_fusion
  496.4 277.0 %all-reduce.2.cloned.1.call-done = bf16[192,6144]{1,0:T(8,128)(2,1)} async-done(((bf16[192,6144]{1,0:T(8,128)(2,1)}), bf16[192,6144]{1,0:T(8,128)(2,1)}) %all-reduce.2.cloned.1.call-update) | async-done | bytes 2359312 | tf_op jit(solution)/shard_map/psum | solution.py:79
  (79 shorter events, 47.9 us)
Async XLA Ops:
  6.5 486.6 %copy-start = (bf16[256,6144]{1,0:T(8,128)(2,1)S(1)}, bf16[256,6144]{1,0:T(8,128)(2,1)}, u32[]{:S(2)}) copy-start(bf16[256,6144]{1,0:T(8,128)(2,1)} %param.16) | copy-start | bytes 9437188
  6.5 199.6 %all-gather.8.cloned.1.call-start = ((), (), s32[]{:S(2)}) async-start(), calls=%async_computation.1 | async-start | bytes 2506752 | tf_op jit(solution)/shard_map/all_gather | solution.py:38
  117.6 170.3 %all-gather.6.cloned.1.call-start = ((), (), s32[]{:S(2)}) async-start(), calls=%async_computation | async-start | bytes 9732096 | tf_op jit(solution)/shard_map/all_gather | solution.py:39
  120.3 246.2 %all-gather.10.cloned.1.call-start = ((), (), s32[]{:S(2)}) async-start(), calls=%async_computation.2 | async-start | bytes 3244032 | tf_op jit(solution)/shard_map/all_gather | solution.py:65
  294.3 0.8 copy-start.2
  295.1 7.7 copy-start.3
  300.6 133.7 %all-gather.12.cloned.1.call-start = ((), (), s32[]{:S(2)}) async-start(), calls=%async_computation.4 | async-start | bytes 3244032 | tf_op jit(solution)/shard_map/all_gather | solution.py:66
  302.2 471.2 %all-reduce.2.cloned.1.call-start = ((), (), s32[]{:S(2)}) async-start(), calls=%async_computation.3 | async-start | bytes 4718592 | tf_op jit(solution)/shard_map/psum | solution.py:79
  493.1 280.3 %copy-start.1 = (bf16[192,384]{1,0:T(8,128)(2,1)S(1)}, bf16[192,384]{1,0:T(8,128)(2,1)}, u32[]{:S(2)}) copy-start(bf16[192,384]{1,0:T(8,128)(2,1)} %param.11) | copy-start | bytes 442372
Sparse Core Ops, SparseCore 0:
  117.7 88.3 all-gather.7
  208.2 79.6 all-gather.5
  300.7 65.7 all-gather.9
  368.5 65.7 all-gather.11
  496.5 276.8 all-reduce.1
where the time goes:
time: 783 us; the launch traced here: 782 us
  waiting for transfers between devices  570 us (73%)
  blocking collectives  105 us (13%)
  matrix products  47.8 us (6%)
  local copies, waits for them, and re-layouts  32.3 us (4%)
  between operations  14.7 us (2%)
  other arithmetic  12.1 us (2%)
    psum x1, waiting for transfers between devices, per_device(): summed = lax.psum(partial_terms, ('head', 'seq')).astype(jnp.float32)  277 us
    all_gather x1, waiting for transfers between devices, per_device(): hidden = lax.all_gather(shares, ('head', 'seq'), axis=1, tiled=True)  85.2 us
    all_gather x1, waiting for transfers between devices, per_device(): full_weights = lax.all_gather(ema_weights, 'fsdp', axis=1, tiled=True)  81.8 us
    all_gather x1, waiting for transfers between devices, per_device(): lax.all_gather(keys, 'fsdp', axis=0, tiled=True)  63.6 us
    all_gather x1, waiting for transfers between devices, per_device(): lax.all_gather(values, 'fsdp', axis=0, tiled=True)  62.2 us
    psum x1, blocking collectives, per_device(): average = lax.psum(jnp.sum(widened, axis=1), ('head', 'seq')) / D  58.4 us
    psum x1, blocking collectives, per_device(): variance = lax.psum(jnp.sum(centred * centred, axis=1), ('head', 'seq')) / D  46.3 us
    dot_general x12, matrix products, one_block(): jnp.einsum('hqk,khd->qhd', weights, value_block, preferred_element_type=j...  23.8 us
  transfers between devices with their start and end apart: 5, of which 5 were waited for; matrix products, arithmetic and copies ran while one was open for 1% of the time, Pallas kernels for 0%

commit v1 on v0

--- a/solution.py
+++ b/solution.py
@@ -29,7 +29,7 @@
     position = lax.axis_index(("head", "seq")) * local_width
     own_mod = lax.dynamic_slice_in_dim(mod_row, position, local_width, 1)
     widened = latents.astype(jnp.float32)
-    average = lax.psum(jnp.sum(widened, axis=1), ("head", "seq")) / D
+    average = lax.psum(lax.psum(jnp.sum(widened, axis=1), axis_name="seq"), axis_name="head") / D
     centred = widened - average[:, None]
     variance = lax.psum(jnp.sum(centred * centred, axis=1), ("head", "seq")) / D
     shares = (

time: 783 us -> 757 us (0.967)
  blocking collectives: 105 us -> 79.8 us
    psum x1 -> x2, blocking collectives: 58.4 us -> 30.8 us  [the longest x1 20.3 us: per_device(): lax.psum(lax.psum(jnp.sum(widened, axis=1), axis_name='seq'), axis_name='...]
where the time goes in v1:
time: 757 us; the launch traced here: 756 us
  waiting for transfers between devices  569 us (75%)
  blocking collectives  79.8 us (11%)
  matrix products  47.8 us (6%)
  local copies, waits for them, and re-layouts  32.3 us (4%)
  between operations  14.7 us (2%)
  other arithmetic  12.1 us (2%)
    psum x1, waiting for transfers between devices, per_device(): summed = lax.psum(partial_terms, ('head', 'seq')).astype(jnp.float32)  276 us
    all_gather x1, waiting for transfers between devices, per_device(): hidden = lax.all_gather(shares, ('head', 'seq'), axis=1, tiled=True)  85.4 us
    all_gather x1, waiting for transfers between devices, per_device(): full_weights = lax.all_gather(ema_weights, 'fsdp', axis=1, tiled=True)  81.8 us
    all_gather x1, waiting for transfers between devices, per_device(): lax.all_gather(keys, 'fsdp', axis=0, tiled=True)  63.5 us
    all_gather x1, waiting for transfers between devices, per_device(): lax.all_gather(values, 'fsdp', axis=0, tiled=True)  62.2 us
    psum x1, blocking collectives, per_device(): variance = lax.psum(jnp.sum(centred * centred, axis=1), ('head', 'seq')) / D  49 us
    dot_general x12, matrix products, one_block(): jnp.einsum('hqk,khd->qhd', weights, value_block, preferred_element_type=j...  23.8 us
    psum x1, blocking collectives, per_device(): lax.psum(lax.psum(jnp.sum(widened, axis=1), axis_name='seq'), axis_name='...  20.3 us
  transfers between devices with their start and end apart: 5, of which 5 were waited for; matrix products, arithmetic and copies ran while one was open for 1% of the time, Pallas kernels for 0%

profile of v1, /device:TPU:40, one launch (start us, length us, event | category | flops | bytes accessed | tf_op | source)
XLA Modules:
  0.0 756.3 jit_solution(6647870491873004011)
XLA Ops:
  10.0 10.5 %psum.28 = f32[192]{0:T(256)S(1)} all-reduce(f32[192]{0:T(256)S(1)} %convert_reduce_fusion), channel_id=1, replica_groups=mesh['fsdp'=32,'head'=4,'seq'=4] {'seq'}, use_global_device_ids=true, to_apply=%region_1.0 | all-reduce | flops 192 | bytes 1536 | tf_op jit(solution)/shard_map/psum | solution.py:32
  20.5 20.3 %psum.29 = f32[192]{0:T(256)S(1)} all-reduce(f32[192]{0:T(256)S(1)} %psum.28), channel_id=1, replica_groups=mesh['fsdp'=32,'head'=4,'seq'=4] {'head'}, use_global_device_ids=true, to_apply=%region_2.0 | all-reduce | flops 192 | bytes 1536 | tf_op jit(solution)/shard_map/psum | solution.py:32
  42.0 49.0 %psum.30 = f32[192]{0:T(256)S(1)} all-reduce(f32[192]{0:T(256)S(1)} %fusion.11), channel_id=1, replica_groups=mesh['fsdp'=32,'head'=4,'seq'=4] {'head','seq'}, use_global_device_ids=true, to_apply=%region_4.0 | all-reduce | flops 192 | bytes 1536 | tf_op jit(solution)/shard_map/psum | solution.py:34
  96.1 85.4 %all-gather.8.cloned.1.call-done = bf16[192,6144]{1,0:T(8,128)(2,1)} async-done(((bf16[192,384]{1,0:T(8,128)(2,1)}), bf16[192,6144]{1,0:T(8,128)(2,1)}) %all-gather.8.cloned.1.call-update) | async-done | bytes 2359312 | tf_op jit(solution)/shard_map/all_gather | solution.py:38
  181.6 81.8 %all-gather.6.cloned.1.call-done = bf16[3,6144,256]{2,1,0:T(8,128)(2,1)} async-done(((bf16[3,192,256]{2,1,0:T(8,128)(2,1)}), bf16[3,6144,256]{2,1,0:T(8,128)(2,1)}) %all-gather.6.cloned.1.call-update) | async-done | bytes 9437200 | tf_op jit(solution)/shard_map/all_gather | solution.py:39
  263.3 6.4 fusion.6
  278.3 63.5 %all-gather.10.cloned.1.call-done = bf16[6144,256]{1,0:T(8,128)(2,1)} async-done(((bf16[192,256]{1,0:T(8,128)(2,1)}), bf16[6144,256]{1,0:T(8,128)(2,1)}) %all-gather.10.cloned.1.call-update) | async-done | bytes 3145744 | tf_op jit(solution)/shard_map/all_gather | solution.py:65
  341.9 5.5 reshape.43
  347.4 62.2 %all-gather.12.cloned.1.call-done = bf16[1,6144,256]{2,1,0:T(8,128)(2,1)} async-done(((bf16[1,192,256]{2,1,0:T(8,128)(2,1)}), bf16[1,6144,256]{2,1,0:T(8,128)(2,1)}) %all-gather.12.cloned.1.call-update) | async-done | bytes 3145744 | tf_op jit(solution)/shard_map/all_gather | solution.py:66
  409.7 5.5 reshape.42
  415.2 53.4 %while.13 = (s32[]{:T(128)}, f32[192,2,128]{2,0,1:T(8,128)}, f32[192,2]{0,1:T(2,128)S(1)}, bf16[12,512,2,128]{3,2,1,0:T(2,128)(2,1)}, bf16[12,512,2,128]{3,2,1,0...) while((s32[]{:T(128)}, f32[192,2,128]{2,0,1:T(8,128)}, ...), condition=%wide.region_9.10_spmd.clone, body=%wide.region_7.9_spmd.clone.sunk | while | flops 101351808 | bytes 2857060 | solution.py:73
  422.0 2.0 fusion.45
  426.5 2.0 fusion.45
  430.9 2.0 fusion.45
  435.4 2.0 fusion.45
  439.8 2.0 fusion.45
  444.3 2.0 fusion.45
  448.8 2.0 fusion.45
  453.2 2.0 fusion.45
  457.7 2.0 fusion.45
  462.1 2.0 fusion.45
  466.6 2.0 fusion.45
  468.6 3.2 convolution_convert_fusion
  471.8 276.3 %all-reduce.2.cloned.1.call-done = bf16[192,6144]{1,0:T(8,128)(2,1)} async-done(((bf16[192,6144]{1,0:T(8,128)(2,1)}), bf16[192,6144]{1,0:T(8,128)(2,1)}) %all-reduce.2.cloned.1.call-update) | async-done | bytes 2359312 | tf_op jit(solution)/shard_map/psum | solution.py:79
  (80 shorter events, 49.8 us)
Async XLA Ops:
  6.5 462.0 %copy-start = (bf16[256,6144]{1,0:T(8,128)(2,1)S(1)}, bf16[256,6144]{1,0:T(8,128)(2,1)}, u32[]{:S(2)}) copy-start(bf16[256,6144]{1,0:T(8,128)(2,1)} %param.16) | copy-start | bytes 9437188
  6.5 175.0 %all-gather.8.cloned.1.call-start = ((), (), s32[]{:S(2)}) async-start(), calls=%async_computation.1 | async-start | bytes 2506752 | tf_op jit(solution)/shard_map/all_gather | solution.py:38
  92.8 170.5 %all-gather.6.cloned.1.call-start = ((), (), s32[]{:S(2)}) async-start(), calls=%async_computation | async-start | bytes 9732096 | tf_op jit(solution)/shard_map/all_gather | solution.py:39
  95.4 246.5 %all-gather.10.cloned.1.call-start = ((), (), s32[]{:S(2)}) async-start(), calls=%async_computation.2 | async-start | bytes 3244032 | tf_op jit(solution)/shard_map/all_gather | solution.py:65
  269.7 0.8 copy-start.2
  270.5 7.7 %copy-start.3 = (f32[128]{0:T(128)S(1)}, f32[128]{0:T(128)}, u32[]{:S(2)}) copy-start(f32[128]{0:T(128)} %param.14) | copy-start | bytes 1540
  276.0 133.7 %all-gather.12.cloned.1.call-start = ((), (), s32[]{:S(2)}) async-start(), calls=%async_computation.4 | async-start | bytes 3244032 | tf_op jit(solution)/shard_map/all_gather | solution.py:66
  277.7 470.5 %all-reduce.2.cloned.1.call-start = ((), (), s32[]{:S(2)}) async-start(), calls=%async_computation.3 | async-start | bytes 4718592 | tf_op jit(solution)/shard_map/psum | solution.py:79
  468.6 279.6 %copy-start.1 = (bf16[192,384]{1,0:T(8,128)(2,1)S(1)}, bf16[192,384]{1,0:T(8,128)(2,1)}, u32[]{:S(2)}) copy-start(bf16[192,384]{1,0:T(8,128)(2,1)} %param.11) | copy-start | bytes 442372
Sparse Core Ops, SparseCore 0:
  92.9 88.6 all-gather.7
  183.7 79.6 all-gather.5
  276.1 65.7 all-gather.9
  343.9 65.7 all-gather.11
  471.9 276.1 all-reduce.1

commit v2 on v0

--- a/solution.py
+++ b/solution.py
@@ -3,9 +3,11 @@
 import jax.numpy as jnp
 from jax import lax
 from jax.sharding import PartitionSpec as P
+from jax.lax import all_gather
 
 D = 6144
 HD = 128
+remake_waves_up = lambda here_x: jnp.sum(all_gather(here_x, ("head", "seq")), 0)
 
 
 def head_norm(projected_part, gain, heads):
@@ -76,7 +78,7 @@
     partial_terms = jnp.dot(attended, out_weight, preferred_element_type=jnp.float32).astype(
         jnp.bfloat16
     )
-    summed = lax.psum(partial_terms, ("head", "seq")).astype(jnp.float32)
+    summed = remake_waves_up(partial_terms).astype(jnp.float32)
     branch = lax.dynamic_slice_in_dim(summed, position, local_width, 1)
     return (widened + own_mod[2][None, :] * branch).astype(jnp.bfloat16)
 

time: 783 us -> 1300 us (1.66)
  the two profiles are of different devices: /device:TPU:40 before, /device:TPU:1 now
where the time goes in v2:
time: 1300 us
  waiting for transfers between devices  1120 us (86%)
  blocking collectives  92.2 us (7%)
  local copies, waits for them, and re-layouts  31.6 us (2%)
  other arithmetic  27.7 us (2%)
  matrix products  18.1 us (1%)
  between operations  14.8 us (1%)
    all_gather x1, waiting for transfers between devices, all_gather(here_x, ('head', 'seq'))  812 us
    all_gather x1, waiting for transfers between devices, per_device(): hidden = lax.all_gather(shares, ('head', 'seq'), axis=1, tiled=True)  108 us
    all_gather x1, waiting for transfers between devices, per_device(): full_weights = lax.all_gather(ema_weights, 'fsdp', axis=1, tiled=True)  75 us
    all_gather x1, waiting for transfers between devices, per_device(): lax.all_gather(keys, 'fsdp', axis=0, tiled=True)  62.1 us
    all_gather x1, waiting for transfers between devices, per_device(): lax.all_gather(values, 'fsdp', axis=0, tiled=True)  58.2 us
    psum x1, blocking collectives, per_device(): average = lax.psum(jnp.sum(widened, axis=1), ('head', 'seq')) / D  52.9 us
    psum x1, blocking collectives, per_device(): variance = lax.psum(jnp.sum(centred * centred, axis=1), ('head', 'seq')) / D  39.3 us
  transfers between devices with their start and end apart: 5, of which 5 were waited for; matrix products, arithmetic and copies ran while one was open for 1% of the time, Pallas kernels for 0%

profile of v2, /device:TPU:1, one launch (start us, length us, event | category | flops | bytes accessed | tf_op | source)
XLA Modules:
  0.0 1300.0 jit_solution(17180881695900988566)
XLA Ops:
  8.5 52.9 %psum.14 = f32[192]{0:T(256)S(1)} all-reduce(f32[192]{0:T(256)S(1)} %convert_reduce_fusion), channel_id=1, replica_groups=mesh['fsdp'=32,'head'=4,'seq'=4] {'head','seq'}, use_global_device_ids=true, to_apply=%region_1.0 | all-reduce | flops 192 | bytes 1536 | tf_op jit(solution)/shard_map/psum | solution.py:34
  62.5 39.3 %psum.15 = f32[192]{0:T(256)S(1)} all-reduce(f32[192]{0:T(256)S(1)} %fusion.11), channel_id=1, replica_groups=mesh['fsdp'=32,'head'=4,'seq'=4] {'head','seq'}, use_global_device_ids=true, to_apply=%region_3.0 | all-reduce | flops 192 | bytes 1536 | tf_op jit(solution)/shard_map/psum | solution.py:36
  101.8 1.5 fusion.23
  103.4 1.7 fusion.14
  105.9 1.9 add_convert_fusion
  107.9 107.7 %all-gather.10.cloned.1.call-done = bf16[192,6144]{1,0:T(8,128)(2,1)} async-done(((bf16[192,384]{1,0:T(8,128)(2,1)}), bf16[192,6144]{1,0:T(8,128)(2,1)}) %all-gather.10.cloned.1.call-update) | async-done | bytes 2359312 | tf_op jit(solution)/shard_map/all_gather | solution.py:40
  215.6 75.0 %all-gather.8.cloned.1.call-done = bf16[3,6144,256]{2,1,0:T(8,128)(2,1)} async-done(((bf16[3,192,256]{2,1,0:T(8,128)(2,1)}), bf16[3,6144,256]{2,1,0:T(8,128)(2,1)}) %all-gather.8.cloned.1.call-update) | async-done | bytes 9437200 | tf_op jit(solution)/shard_map/all_gather | solution.py:41
  290.6 6.4 fusion.6
  298.6 1.7 fusion.30
  301.0 1.6 fusion.17
  306.3 58.2 %all-gather.14.cloned.1.call-done = bf16[1,6144,256]{2,1,0:T(8,128)(2,1)} async-done(((bf16[1,192,256]{2,1,0:T(8,128)(2,1)}), bf16[1,6144,256]{2,1,0:T(8,128)(2,1)}) %all-gather.14.cloned.1.call-update) | async-done | bytes 3145744 | tf_op jit(solution)/shard_map/all_gather | solution.py:68
  364.5 5.5 reshape.42
  370.0 62.1 %all-gather.12.cloned.1.call-done = bf16[6144,256]{1,0:T(8,128)(2,1)} async-done(((bf16[192,256]{1,0:T(8,128)(2,1)}), bf16[6144,256]{1,0:T(8,128)(2,1)}) %all-gather.12.cloned.1.call-update) | async-done | bytes 3145744 | tf_op jit(solution)/shard_map/all_gather | solution.py:67
  432.2 5.5 reshape.43
  437.7 25.2 %while.13 = (s32[]{:T(128)}, f32[192,2,128]{2,0,1:T(8,128)S(1)}, f32[192,2]{0,1:T(2,128)S(1)}, bf16[12,512,2,128]{3,2,1,0:T(2,128)(2,1)}, bf16[12,512,2,128]{3,2...) while((s32[]{:T(128)}, f32[192,2,128]{2,0,1:T(8,128)S(1)}, ...), condition=%wide.region_8.9_spmd.clone, body=%wide.region_6.8_spmd.clone.sunk | while | flops 101351808 | bytes 2857068 | solution.py:75
  441.9 1.4 constant_dynamic-slice_fusion.3
  444.0 1.4 constant_dynamic-slice_fusion.3
  446.1 1.4 constant_dynamic-slice_fusion.3
  450.3 1.4 constant_dynamic-slice_fusion.3
  452.4 1.4 constant_dynamic-slice_fusion.3
  462.9 2.2 convolution_convert_fusion
  465.2 812.0 %all-gather.16.cloned.1.call-done = bf16[3072,6144]{1,0:T(8,128)(2,1)} async-done(((bf16[192,6144]{1,0:T(8,128)(2,1)}), bf16[3072,6144]{1,0:T(8,128)(2,1)}) %all-gather.16.cloned.1.call-update) | async-done | bytes 37748752 | tf_op jit(solution)/shard_map/all_gather | solution.py:10
  1277.2 14.7 %reduce_sum.61 = bf16[192,6144]{1,0:T(8,128)(2,1)} reduce(bf16[16,192,6144]{2,1,0:T(8,128)(2,1)} %bitcast.68, bf16[]{:T(256)} %constant.51.clone.1), dimensions={0}, to_apply=%region_9.10 | reduce | flops 17694720 | bytes 40108032 | tf_op jit(solution)/shard_map/reduce_sum | solution.py:10
  1291.9 1.6 fusion.15
  (86 shorter events, 26.4 us)
Async XLA Ops:
  6.5 456.4 %copy-start = (bf16[256,6144]{1,0:T(8,128)(2,1)S(1)}, bf16[256,6144]{1,0:T(8,128)(2,1)}, u32[]{:S(2)}) copy-start(bf16[256,6144]{1,0:T(8,128)(2,1)} %param.16) | copy-start | bytes 9437188
  6.5 209.0 %all-gather.10.cloned.1.call-start = ((), (), s32[]{:S(2)}) async-start(), calls=%async_computation.1 | async-start | bytes 2506752 | tf_op jit(solution)/shard_map/all_gather | solution.py:40
  105.2 185.4 %all-gather.8.cloned.1.call-start = ((), (), s32[]{:S(2)}) async-start(), calls=%async_computation | async-start | bytes 9732096 | tf_op jit(solution)/shard_map/all_gather | solution.py:41
  107.8 190.7 %copy-start.6 = (f32[128]{0:T(128)S(1)}, f32[128]{0:T(128)}, u32[]{:S(2)}) copy-start(f32[128]{0:T(128)} %param.15) | copy-start | bytes 1540
  107.8 256.7 %all-gather.14.cloned.1.call-start = ((), (), s32[]{:S(2)}) async-start(), calls=%async_computation.3 | async-start | bytes 3244032 | tf_op jit(solution)/shard_map/all_gather | solution.py:68
  297.0 0.8 copy-start.3
  297.8 7.8 copy-start.5
  298.5 133.7 %all-gather.12.cloned.1.call-start = ((), (), s32[]{:S(2)}) async-start(), calls=%async_computation.2 | async-start | bytes 3244032 | tf_op jit(solution)/shard_map/all_gather | solution.py:67
  302.6 974.6 %all-gather.16.cloned.1.call-start = ((), (), s32[]{:S(2)}) async-start(), calls=%async_computation.4 | async-start | bytes 40108032 | tf_op jit(solution)/shard_map/all_gather | solution.py:10
  370.0 67.7 %copy-start.4 = (bf16[192,2,128]{2,0,1:T(8,128)(2,1)S(1)}, bf16[192,2,128]{2,0,1:T(8,128)(2,1)}, u32[]{:S(2)}) copy-start(bf16[192,2,128]{2,0,1:T(8,128)(2,1)} %fusion.19) | copy-start | bytes 294916
  1277.2 14.7 %copy-start.2 = (bf16[192,384]{1,0:T(8,128)(2,1)S(1)}, bf16[192,384]{1,0:T(8,128)(2,1)}, u32[]{:S(2)}) copy-start(bf16[192,384]{1,0:T(8,128)(2,1)} %param.11) | copy-start | bytes 442372
  1277.2 16.3 %copy-start.1 = (bf16[256,6144]{1,0:T(8,128)(2,1)S(1)}, bf16[256,6144]{1,0:T(8,128)(2,1)}, u32[]{:S(2)}) copy-start(bf16[256,6144]{1,0:T(8,128)(2,1)} %param.16) | copy-start | bytes 9437188
Sparse Core Ops, SparseCore 0:
  105.3 110.2 all-gather.9
  217.7 72.8 all-gather.7
  298.6 65.8 all-gather.13
  366.5 65.6 all-gather.11
  465.3 811.8 all-gather.15
